TPU v7x, 32 devices: a whole 2x2x4 slice. The times are simulated.
32 devices in a mesh: dp: 4 (over x, core), group: 8 (over z, y).
Axes of the slice: x: 2, y: 2, z: 4, core: 2. Of those that a mesh axis runs over, the one named last changes fastest.
Arguments:
- image_tiles: bfloat16 [4, 8, 8, 4, 4, 352], P('dp', 'group'), may hold values from -6 to 6
- cotangent: bfloat16 [4, 8, 8, 4, 4, 352], P('dp', 'group'), may hold values from -6 to 6
- image_rows: int32 [4, 8], P('dp', 'group'), may hold values from 1 to 2, as said below
- dw_kernel: float32 [7, 7, 352], replicated, may hold values from -0.875 to 0.875
- dw_bias: float32 [352], replicated, may hold values from -1 to 1
- layer_norm_gain: float32 [352], replicated, may hold values from 0.1 to 1.9
- layer_norm_bias: float32 [352], replicated, may hold values from -3 to 3
- weight_in: bfloat16 [352, 1408], replicated, may hold values from -0.3125 to 0.3125
- bias_in: float32 [1408], replicated, may hold values from -2.5 to 1
- grn_gamma: float32 [1408], replicated, may hold values from -1 to 1
- grn_beta: float32 [1408], replicated, may hold values from -3 to 3
- weight_out: bfloat16 [1408, 352], replicated, may hold values from -0.15625 to 0.15625
- bias_out: float32 [352], replicated, may hold values from -3 to 3
Outputs:
- outputs: bfloat16 [4, 8, 8, 4, 4, 352], P('dp', 'group')
- input_grads: bfloat16 [4, 8, 8, 4, 4, 352], P('dp', 'group')
- grad_shards: float32 [32, 31696], P(('dp', 'group'))
Inputs may be any that keep to these rules, and one draw needn't show every extreme that they name: `image_rows`: some device's image has all 2 tile rows.
All inputs are finite; a program needn't handle non-finite values.
Results may differ from a plain program's by a relative error of at most 0.0051.
Values may be sent and summed in bfloat16 or wider, within the bound.
No kernel may reach another device: no remote copies, remote signals or barrier semaphores. Data moves between devices by JAX's collectives and lax.ppermute only.
A program may use at most 64 MiB of HBM per device.

v0:
```python
import math
import jax
import jax.numpy as jnp
from jax import lax
from jax.sharding import PartitionSpec as P

GC = 4


def image_step(
    inputs,
    upstream,
    valid,
    dw_kernel,
    dw_bias,
    layer_norm_gain,
    layer_norm_bias,
    weight_in,
    bias_in,
    grn_gamma,
    grn_beta,
    weight_out,
    bias_out,
):
    height, width, channel_count = inputs.shape
    hidden_dim = weight_in.shape[1]
    total_row_count = height * width
    cell_mask = jnp.broadcast_to(valid, (height, width, 1)).reshape(total_row_count, 1)
    float_in = inputs.astype(jnp.float32)
    padded_in = jnp.pad(float_in, ((3, 3), (3, 3), (0, 0)))
    conv_out = jnp.zeros_like(float_in) + dw_bias
    for row_off in range(7):
        for col_off in range(7):
            conv_out = (
                conv_out
                + padded_in[row_off : row_off + height, col_off : col_off + width, :]
                * dw_kernel[row_off, col_off]
            )
    mean_c = jnp.mean(conv_out, axis=-1, keepdims=True)
    centered_values = conv_out - mean_c
    inverse_deviation = lax.rsqrt(
        jnp.mean(centered_values * centered_values, axis=-1, keepdims=True) + 1e-06
    )
    standardized_input = centered_values * inverse_deviation
    normalized_output = (
        (standardized_input * layer_norm_gain + layer_norm_bias)
        .astype(jnp.bfloat16)
        .reshape(total_row_count, channel_count)
    )
    pre_act = jnp.dot(normalized_output, weight_in, preferred_element_type=jnp.float32) + bias_in
    act_out = 0.5 * pre_act * (1.0 + lax.erf(pre_act * 0.7071067811865476))
    act_kept = act_out * cell_mask
    norm_val = jnp.sqrt(1.0 + jnp.sum(act_kept * act_kept, axis=0, keepdims=True))
    denom = jnp.mean(norm_val, axis=-1, keepdims=True) + 1e-06
    scale_val = norm_val / denom
    mixed = (grn_gamma * (act_out * scale_val) + grn_beta + act_out).astype(jnp.bfloat16)
    branch = jnp.dot(mixed, weight_out, preferred_element_type=jnp.float32) + bias_out
    whole = float_in.reshape(total_row_count, channel_count) + branch
    result = (
        jnp.where(cell_mask > 0, whole, jnp.zeros_like(whole))
        .astype(jnp.bfloat16)
        .reshape(inputs.shape)
    )
    up_rows = upstream.reshape(total_row_count, channel_count)
    up_float = up_rows.astype(jnp.float32)
    g_bias_out = jnp.sum(up_float, axis=0)
    g_weight_out = lax.dot_general(
        mixed, up_rows, (((0,), (0,)), ((), ())), preferred_element_type=jnp.float32
    )
    d_mixed = lax.dot_general(
        up_rows, weight_out, (((1,), (1,)), ((), ())), preferred_element_type=jnp.float32
    )
    g_gamma = jnp.sum(d_mixed * act_out * scale_val, axis=0)
    g_beta = jnp.sum(d_mixed, axis=0)
    d_scale = jnp.sum(d_mixed * grn_gamma * act_out, axis=0, keepdims=True)
    d_norm = (
        d_scale / denom
        - jnp.sum(d_scale * norm_val, axis=-1, keepdims=True) / (denom * denom) / hidden_dim
    )
    d_act = d_mixed * (grn_gamma * scale_val + 1.0) + act_kept * d_norm / norm_val
    cdf_val = 0.5 * (1.0 + lax.erf(pre_act * 0.7071067811865476))
    pdf_val = jnp.exp(-0.5 * pre_act * pre_act) * 0.3989422804014327
    d_pre = d_act * (cdf_val + pre_act * pdf_val)
    g_bias_in = jnp.sum(d_pre, axis=0)
    d_pre_b = d_pre.astype(jnp.bfloat16)
    g_weight_in = lax.dot_general(
        normalized_output, d_pre_b, (((0,), (0,)), ((), ())), preferred_element_type=jnp.float32
    )
    normalized_gradient = lax.dot_general(
        d_pre_b, weight_in, (((1,), (1,)), ((), ())), preferred_element_type=jnp.float32
    ).reshape(inputs.shape)
    layer_norm_gain_gradient = jnp.sum(normalized_gradient * standardized_input, axis=(0, 1))
    g_ln_bias = jnp.sum(normalized_gradient, axis=(0, 1))
    upscaled_values = normalized_gradient * layer_norm_gain
    conv_output_gradient = inverse_deviation * (
        upscaled_values
        - jnp.mean(upscaled_values, axis=-1, keepdims=True)
        - standardized_input
        * jnp.mean(upscaled_values * standardized_input, axis=-1, keepdims=True)
    )
    g_dw_bias = jnp.sum(conv_output_gradient, axis=(0, 1))
    padded_grad = jnp.pad(conv_output_gradient, ((3, 3), (3, 3), (0, 0)))
    back_float = up_float.reshape(inputs.shape)
    kernel_rows = []
    for row_off in range(7):
        for col_off in range(7):
            kernel_rows.append(
                jnp.sum(
                    padded_in[row_off : row_off + height, col_off : col_off + width, :]
                    * conv_output_gradient,
                    axis=(0, 1),
                )
            )
            back_float = (
                back_float
                + padded_grad[
                    6 - row_off : 6 - row_off + height, 6 - col_off : 6 - col_off + width, :
                ]
                * dw_kernel[row_off, col_off]
            )
    back_float = jnp.where(valid > 0, back_float, jnp.zeros_like(back_float))
    g_kernel = jnp.stack(kernel_rows)
    grad_flat = jnp.concatenate(
        [
            g_kernel.reshape(-1),
            g_dw_bias,
            layer_norm_gain_gradient,
            g_ln_bias,
            g_weight_in.reshape(-1),
            g_bias_in,
            g_gamma,
            g_beta,
            g_weight_out.reshape(-1),
            g_bias_out,
        ]
    )
    return (result, back_float.astype(jnp.bfloat16), grad_flat)


def to_canvas(tiles, grid_rows, grid_cols):
    slot_count, tile_h, tile_w, channel_count = tiles.shape
    return (
        tiles.reshape(grid_rows, grid_cols, tile_h, tile_w, channel_count)
        .transpose(0, 2, 1, 3, 4)
        .reshape(grid_rows * tile_h, grid_cols * tile_w, channel_count)
    )


def to_tiles(canvas, grid_rows, grid_cols, tile_h, tile_w):
    channel_count = canvas.shape[-1]
    return (
        canvas.reshape(grid_rows, tile_h, grid_cols, tile_w, channel_count)
        .transpose(0, 2, 1, 3, 4)
        .reshape(grid_rows * grid_cols, tile_h, tile_w, channel_count)
    )


def per_device(
    image_tiles,
    cotangent,
    image_rows,
    dw_kernel,
    dw_bias,
    layer_norm_gain,
    layer_norm_bias,
    weight_in,
    bias_in,
    grn_gamma,
    grn_beta,
    weight_out,
    bias_out,
):
    received = lax.all_to_all(image_tiles, "group", split_axis=2, concat_axis=2, tiled=True)
    tiles = received[0, 0]
    slot_count, tile_h, tile_w, channel_count = tiles.shape
    grid_rows = slot_count // GC
    cell_rows = jnp.arange(grid_rows * tile_h, dtype=jnp.int32) // tile_h
    valid = (cell_rows < image_rows[0, 0]).astype(jnp.float32).reshape(grid_rows * tile_h, 1, 1)
    canvas = to_canvas(tiles, grid_rows, GC)
    canvas = jnp.where(valid > 0, canvas, jnp.zeros_like(canvas))
    up_canvas = to_canvas(cotangent[0, 0], grid_rows, GC)
    up_canvas = jnp.where(valid > 0, up_canvas, jnp.zeros_like(up_canvas))
    params = (
        dw_kernel,
        dw_bias,
        layer_norm_gain,
        layer_norm_bias,
        weight_in,
        bias_in,
        grn_gamma,
        grn_beta,
        weight_out,
        bias_out,
    )
    result, back_grads, grad_flat = image_step(canvas, up_canvas, valid, *params)
    outputs = to_tiles(result, grid_rows, GC, tile_h, tile_w)
    back_tiles = to_tiles(back_grads, grid_rows, GC, tile_h, tile_w)
    returned = lax.all_to_all(
        back_tiles[None, None], "group", split_axis=2, concat_axis=2, tiled=True
    )
    data_count = lax.axis_size("dp")
    group_count = lax.axis_size("group")
    devices_all = data_count * group_count
    total_len = grad_flat.shape[0]
    shard_len = (total_len + 8 * devices_all - 1) // (8 * devices_all) * 8
    padded = jnp.pad(grad_flat, (0, devices_all * shard_len - total_len))
    factor = 1.0 / math.sqrt(data_count * group_count * group_count * tile_h * tile_w)
    owned = lax.psum_scatter(
        padded.reshape(devices_all, shard_len), ("dp", "group"), scatter_dimension=0, tiled=True
    )
    return (outputs[None, None], returned, owned * factor)


def solution(mesh):
    return jax.shard_map(
        per_device,
        mesh=mesh,
        in_specs=(
            P("dp", "group", None, None, None, None),
            P("dp", "group", None, None, None, None),
            P("dp", "group"),
            P(),
            P(),
            P(),
            P(),
            P(),
            P(),
            P(),
            P(),
            P(),
            P(),
        ),
        out_specs=(
            P("dp", "group", None, None, None, None),
            P("dp", "group", None, None, None, None),
            P(("dp", "group"), None),
        ),
        check_vma=False,
    )
```

profile of v0, /device:TPU:0, one launch (start us, length us, event | category | flops | bytes accessed | tf_op | source)
XLA Modules:
  0.0 254.1 jit_solution(9716714760860221564)
XLA Ops:
  7.2 7.5 %all-to-all-start = ((bf16[1,1,8,4,4,352]{5,4,3,1,0,2:T(4,128)(2,1)}), bf16[1,1,8,4,4,352]{5,4,3,1,0,2:T(4,128)(2,1)S(1)}, u32[]{:S(2)}, u32[]{:S(2)}) async-start(bf16[1,1,8,4,4,352]{5,4,3,1,0,2:T(4,128)(2,1)} %bitcast.47), calls=%async_computation | async-start | bytes 196608 | tf_op jit(solution)/shard_map/all_to_all | solution.py:173
  14.7 1.0 slice_reduce_fusion.46
  15.8 1.3 slice_reduce_fusion.48
  17.2 1.9 slice_reduce_fusion.47
  22.3 0.9 copy.53
  23.4 1.6 convert_reduce_fusion
  25.8 2.2 fusion.123
  28.6 1.1 multiply_reduce_fusion.2
  31.1 2.5 %multiply_reduce_fusion = (f32[1408]{0:T(1024)S(1)}, f32[1408]{0:T(1024)S(1)}, f32[1408]{0:T(1024)S(1)}, f32[128,1408]{1,0:T(8,128)}) fusion(f32[128,1408]{1,0:T(8,128)S(1)} %get-tuple-element.130, f32[1408]{0:T(1024)S(1)} %get-tuple-element.128, f32[1408]{0:T(1024)S(1)} %copy-done.5, bf16[1408,352]{0,1:T(8,128)(2,1)} %param.24, ...), kind=kOutput, calls=%fused_computation.107 | convolution fusion | flops 128180096 | bytes 2551424 | tf_op jit(solution)/shard_map/dot_general | solution.py:70
  35.0 1.6 fusion.121
  38.2 0.9 fusion.119
  39.5 1.7 fusion.107
  42.1 2.8 %reshape.176 = f32[495616]{0:T(1024)} reshape(f32[352,1408]{1,0:T(8,128)} %fusion.107) | data formatting | bytes 3964928 | tf_op jit(solution)/shard_map/reshape | solution.py:129
  44.9 2.5 fusion.111
  47.4 4.0 %reshape.177 = f32[495616]{0:T(1024)} reshape(f32[1408,352]{1,0:T(8,128)} %fusion.111) | data formatting | bytes 3964928 | tf_op jit(solution)/shard_map/reshape | solution.py:133
  51.3 37.9 %concatenate.3 = f32[1014112]{0:T(1024)} concatenate(f32[17248]{0:T(1024)S(1)} %reshape.175, f32[352]{0:T(512)S(1)} %get-tuple-element.59, f32[352]{0:T(512)S(1)} %get-tuple-element.57, f32[352]{0:T(512)S(1)} %get-tuple-element.73, f32[495616]{0:T(1024)} %reshape.176, f32[1408]{0:T(1024)S(1)} %get-tuple-element.124, f32[1408]{0:T(1024)S(1)} %get-tuple-element.6, ...), dimensions={0} | concatenate | bytes 8112896 | tf_op jit(solution)/shard_map/concatenate | solution.py:123
  89.2 4.3 %pad.13 = f32[1014272]{0:T(1024)} pad(f32[1014112]{0:T(1024)} %concatenate.3, f32[]{:T(128)} %constant.50.clone.1), padding=0_160 | pad | bytes 8113540 | tf_op jit(solution)/shard_map/jit(_pad)/pad | solution.py:206
  93.5 6.4 %reshape.178 = f32[32,31696]{1,0:T(8,128)} reshape(f32[1014272]{0:T(1024)} %pad.13) | data formatting | bytes 8114176 | tf_op jit(solution)/shard_map/reshape | solution.py:209
  101.6 2.1 fusion.100
  104.4 6.0 %all-to-all-start.1 = ((bf16[1,1,8,4,4,352]{5,4,3,1,0,2:T(4,128)(2,1)}), bf16[1,1,8,4,4,352]{5,4,3,1,0,2:T(4,128)(2,1)S(1)}, u32[]{:S(2)}, u32[]{:S(2)}) async-start(bf16[1,1,8,4,4,352]{5,4,3,1,0,2:T(4,128)(2,1)} %bitcast.12), calls=%async_computation.1 | async-start | bytes 196608 | tf_op jit(solution)/shard_map/all_to_all | solution.py:198
  110.3 1.7 fusion.2
  112.9 5.8 %all-to-all-done.1 = bf16[1,1,8,4,4,352]{5,4,3,1,0,2:T(4,128)(2,1)S(1)} async-done(((bf16[1,1,8,4,4,352]{5,4,3,1,0,2:T(4,128)(2,1)}), bf16[1,1,8,4,4,352]{5,4,3,1,0,2:T(4,128)(2,1)S(1)}, u32[]{:S(2)}, u32[]{:S(2)}) %all-to-all-start.1) | async-done | bytes 90144 | tf_op jit(solution)/shard_map/all_to_all | solution.py:198
  118.7 125.9 %all-reduce.6.cloned.1.call-done = f32[32,31696]{1,0:T(8,128)} async-done(((f32[32,31696]{1,0:T(8,128)}), f32[32,31696]{1,0:T(8,128)}) %all-reduce.6.cloned.1.call-update) | async-done | bytes 4057104
  244.6 2.0 dynamic-slice_multiply_fusion
  (263 shorter events, 11.0 us)
Async XLA Ops:
  7.2 21.4 %copy-start = (bf16[352,1408]{1,0:T(8,128)(2,1)S(1)}, bf16[352,1408]{1,0:T(8,128)(2,1)}, u32[]{:S(2)}) copy-start(bf16[352,1408]{1,0:T(8,128)(2,1)} %param.20) | copy-start | bytes 2973700
  7.2 21.0 %copy-start.84 = (f32[352]{0:T(512)S(1)}, f32[352]{0:T(512)}, u32[]{:S(2)}) copy-start(f32[352]{0:T(512)} %param.19) | copy-start | bytes 4228
  7.2 21.0 %copy-start.6 = (f32[352]{0:T(512)S(1)}, f32[352]{0:T(512)}, u32[]{:S(2)}) copy-start(f32[352]{0:T(512)} %param.18) | copy-start | bytes 4228
  7.2 21.4 %copy-start.81 = (f32[1408]{0:T(1024)S(1)}, f32[1408]{0:T(1024)}, u32[]{:S(2)}) copy-start(f32[1408]{0:T(1024)} %param.21) | copy-start | bytes 16900
  7.2 17.8 %all-to-all-start = ((bf16[1,1,8,4,4,352]{5,4,3,1,0,2:T(4,128)(2,1)}), bf16[1,1,8,4,4,352]{5,4,3,1,0,2:T(4,128)(2,1)S(1)}, u32[]{:S(2)}, u32[]{:S(2)}) async-start(bf16[1,1,8,4,4,352]{5,4,3,1,0,2:T(4,128)(2,1)} %bitcast.47), calls=%async_computation | async-start | bytes 196608 | tf_op jit(solution)/shard_map/all_to_all | solution.py:173
  14.7 229.9 %all-reduce.6.cloned.1.call-start = ((), (), s32[]{:S(2)}) async-start(), calls=%async_computation.2 | async-start | bytes 8126464
  15.7 12.3 %copy-start.7 = (f32[352]{0:T(512)}, f32[352]{0:T(512)S(1)}, u32[]{:S(2)}) copy-start(f32[352]{0:T(512)S(1)} %get-tuple-element.114) | copy-start | bytes 4228
  15.7 12.3 %copy-start.13 = (f32[352]{0:T(512)}, f32[352]{0:T(512)S(1)}, u32[]{:S(2)}) copy-start(f32[352]{0:T(512)S(1)} %get-tuple-element.117) | copy-start | bytes 4228
  15.7 14.0 %copy-start.9 = (f32[352]{0:T(512)}, f32[352]{0:T(512)S(1)}, u32[]{:S(2)}) copy-start(f32[352]{0:T(512)S(1)} %get-tuple-element.115) | copy-start | bytes 4228
  15.7 14.0 %copy-start.11 = (f32[352]{0:T(512)}, f32[352]{0:T(512)S(1)}, u32[]{:S(2)}) copy-start(f32[352]{0:T(512)S(1)} %get-tuple-element.116) | copy-start | bytes 4228
  15.7 14.0 %copy-start.15 = (f32[352]{0:T(512)}, f32[352]{0:T(512)S(1)}, u32[]{:S(2)}) copy-start(f32[352]{0:T(512)S(1)} %get-tuple-element.118) | copy-start | bytes 4228
  15.7 14.0 %copy-start.17 = (f32[352]{0:T(512)}, f32[352]{0:T(512)S(1)}, u32[]{:S(2)}) copy-start(f32[352]{0:T(512)S(1)} %get-tuple-element.119) | copy-start | bytes 4228
  15.7 14.0 %copy-start.19 = (f32[352]{0:T(512)}, f32[352]{0:T(512)S(1)}, u32[]{:S(2)}) copy-start(f32[352]{0:T(512)S(1)} %get-tuple-element.120) | copy-start | bytes 4228
  15.7 14.0 %copy-start.21 = (f32[352]{0:T(512)}, f32[352]{0:T(512)S(1)}, u32[]{:S(2)}) copy-start(f32[352]{0:T(512)S(1)} %get-tuple-element.121) | copy-start | bytes 4228
  15.8 14.0 %copy-start.23 = (f32[352]{0:T(512)}, f32[352]{0:T(512)S(1)}, u32[]{:S(2)}) copy-start(f32[352]{0:T(512)S(1)} %get-tuple-element.122) | copy-start | bytes 4228
  15.8 14.0 %copy-start.25 = (f32[352]{0:T(512)}, f32[352]{0:T(512)S(1)}, u32[]{:S(2)}) copy-start(f32[352]{0:T(512)S(1)} %get-tuple-element.123) | copy-start | bytes 4228
  17.1 11.3 %copy-start.35 = (f32[352]{0:T(512)}, f32[352]{0:T(512)S(1)}, u32[]{:S(2)}) copy-start(f32[352]{0:T(512)S(1)} %get-tuple-element.79) | copy-start | bytes 4228
  17.1 11.3 %copy-start.37 = (f32[352]{0:T(512)}, f32[352]{0:T(512)S(1)}, u32[]{:S(2)}) copy-start(f32[352]{0:T(512)S(1)} %get-tuple-element.80) | copy-start | bytes 4228
  17.1 11.3 %copy-start.39 = (f32[352]{0:T(512)}, f32[352]{0:T(512)S(1)}, u32[]{:S(2)}) copy-start(f32[352]{0:T(512)S(1)} %get-tuple-element.81) | copy-start | bytes 4228
  17.2 12.6 %copy-start.27 = (f32[352]{0:T(512)}, f32[352]{0:T(512)S(1)}, u32[]{:S(2)}) copy-start(f32[352]{0:T(512)S(1)} %get-tuple-element.75) | copy-start | bytes 4228
  17.2 12.6 %copy-start.29 = (f32[352]{0:T(512)}, f32[352]{0:T(512)S(1)}, u32[]{:S(2)}) copy-start(f32[352]{0:T(512)S(1)} %get-tuple-element.76) | copy-start | bytes 4228
  17.2 12.6 %copy-start.31 = (f32[352]{0:T(512)}, f32[352]{0:T(512)S(1)}, u32[]{:S(2)}) copy-start(f32[352]{0:T(512)S(1)} %get-tuple-element.77) | copy-start | bytes 4228
  17.2 12.6 %copy-start.33 = (f32[352]{0:T(512)}, f32[352]{0:T(512)S(1)}, u32[]{:S(2)}) copy-start(f32[352]{0:T(512)S(1)} %get-tuple-element.78) | copy-start | bytes 4228
  104.4 14.3 %all-to-all-start.1 = ((bf16[1,1,8,4,4,352]{5,4,3,1,0,2:T(4,128)(2,1)}), bf16[1,1,8,4,4,352]{5,4,3,1,0,2:T(4,128)(2,1)S(1)}, u32[]{:S(2)}, u32[]{:S(2)}) async-start(bf16[1,1,8,4,4,352]{5,4,3,1,0,2:T(4,128)(2,1)} %bitcast.12), calls=%async_computation.1 | async-start | bytes 196608 | tf_op jit(solution)/shard_map/all_to_all | solution.py:198
  (65 other events, 298.4 us)
Sparse Core Ops, SparseCore 0:
  100.4 144.1 all-reduce.5
where the time goes:
time: 257 us; the launch traced here: 254 us
  waiting for transfers between devices  132 us (51%)
  local copies, waits for them, and re-layouts  66.1 us (26%)
  between operations  17.7 us (7%)
  other arithmetic  15.1 us (6%)
  starting transfers between devices  13.4 us (5%)
  matrix products  10 us (4%)
    unnamed x2, waiting for transfers between devices  126 us
    concatenate x1, local copies, waits for them, and re-layouts, image_step(): jnp.concatenate([g_kernel.reshape(-1), g_dw_bias, layer_norm_gain_gradien...  37.9 us
    all_to_all x1, starting transfers between devices, per_device(): lax.all_to_all(image_tiles, 'group', split_axis=2, concat_axis=2, tiled=T...  7.45 us
    reshape x1, local copies, waits for them, and re-layouts, per_device(): padded.reshape(devices_all, shard_len)  6.38 us
    all_to_all x1, starting transfers between devices, per_device(): lax.all_to_all(back_tiles[None, None], 'group', split_axis=2, concat_axis...  5.96 us
    all_to_all x1, waiting for transfers between devices, per_device(): lax.all_to_all(back_tiles[None, None], 'group', split_axis=2, concat_axis...  5.82 us
  transfers between devices with their start and end apart: 3, of which 2 were waited for; matrix products, arithmetic and copies ran while one was open for 6% of the time, Pallas kernels for 0%

commit v1 on v0

--- a/solution.py
+++ b/solution.py
@@ -170,7 +170,12 @@
     weight_out,
     bias_out,
 ):
-    received = lax.all_to_all(image_tiles, "group", split_axis=2, concat_axis=2, tiled=True)
+    received = jnp.concatenate(
+        lax.all_to_all(
+            jnp.stack(jnp.split(image_tiles, lax.axis_size("group"), axis=2)), "group", 0, 0
+        ),
+        axis=2,
+    )
     tiles = received[0, 0]
     slot_count, tile_h, tile_w, channel_count = tiles.shape
     grid_rows = slot_count // GC

time: 257 us -> 268 us (1.043)
  local copies, waits for them, and re-layouts: 66.1 us -> 76.7 us
    unnamed x173 -> x180, local copies, waits for them, and re-layouts: 1.01 us -> 10.3 us
where the time goes in v1:
time: 268 us; the launch traced here: 265 us
  waiting for transfers between devices  132 us (49%)
  local copies, waits for them, and re-layouts  76.7 us (29%)
  between operations  17.7 us (7%)
  other arithmetic  15.1 us (6%)
  starting transfers between devices  13.3 us (5%)
  matrix products  10 us (4%)
    unnamed x2, waiting for transfers between devices  126 us
    concatenate x1, local copies, waits for them, and re-layouts, image_step(): jnp.concatenate([g_kernel.reshape(-1), g_dw_bias, layer_norm_gain_gradien...  37.9 us
    unnamed x180, local copies, waits for them, and re-layouts  10.3 us
    all_to_all x1, starting transfers between devices, per_device(): lax.all_to_all(jnp.stack(jnp.split(image_tiles, lax.axis_size('group'), a...  7.31 us
    reshape x1, local copies, waits for them, and re-layouts, per_device(): padded.reshape(devices_all, shard_len)  6.38 us
    all_to_all x1, starting transfers between devices, per_device(): lax.all_to_all(back_tiles[None, None], 'group', split_axis=2, concat_axis...  5.94 us
    all_to_all x1, waiting for transfers between devices, per_device(): lax.all_to_all(back_tiles[None, None], 'group', split_axis=2, concat_axis...  5.82 us
  transfers between devices with their start and end apart: 3, of which 2 were waited for; matrix products, arithmetic and copies ran while one was open for 6% of the time, Pallas kernels for 0%

profile of v1, /device:TPU:0, one launch (start us, length us, event | category | flops | bytes accessed | tf_op | source)
XLA Modules:
  0.0 264.5 jit_solution(10443501598714763003)
XLA Ops:
  7.2 1.4 constant_dynamic-update-slice_fusion.7
  8.6 1.3 constant_dynamic-update-slice_fusion.6
  9.9 1.3 constant_dynamic-update-slice_fusion.5
  11.2 1.3 constant_dynamic-update-slice_fusion.4
  12.5 1.3 constant_dynamic-update-slice_fusion.3
  17.8 7.3 %all-to-all-start = ((bf16[8,1,1,1,4,4,352]{6,5,4,3,2,1,0:T(4,128)(2,1)}), bf16[8,1,1,1,4,4,352]{6,5,4,3,2,1,0:T(4,128)(2,1)S(1)}, u32[]{:S(2)}, u32[]{:S(2)}) async-start(bf16[8,1,1,1,4,4,352]{6,5,4,3,2,1,0:T(4,128)(2,1)} %constant_dynamic-update-slice_fusion), calls=%async_computation | async-start | bytes 196608 | tf_op jit(solution)/shard_map/all_to_all | solution.py:174
  27.7 1.9 slice_reduce_fusion.47
  33.8 1.6 convert_reduce_fusion
  36.3 2.2 fusion.123
  41.6 2.6 multiply_reduce_fusion
  45.4 1.6 fusion.121
  49.9 1.7 fusion.107
  52.5 2.8 %reshape.176 = f32[495616]{0:T(1024)} reshape(f32[352,1408]{1,0:T(8,128)} %fusion.107) | data formatting | bytes 3964928 | tf_op jit(solution)/shard_map/reshape | solution.py:129
  55.3 2.5 fusion.111
  57.8 4.0 %reshape.177 = f32[495616]{0:T(1024)} reshape(f32[1408,352]{1,0:T(8,128)} %fusion.111) | data formatting | bytes 3964928 | tf_op jit(solution)/shard_map/reshape | solution.py:133
  61.8 37.9 %concatenate.3 = f32[1014112]{0:T(1024)} concatenate(f32[17248]{0:T(1024)S(1)} %reshape.175, f32[352]{0:T(512)S(1)} %get-tuple-element.59, f32[352]{0:T(512)S(1)} %get-tuple-element.57, f32[352]{0:T(512)S(1)} %get-tuple-element.73, f32[495616]{0:T(1024)} %reshape.176, f32[1408]{0:T(1024)S(1)} %get-tuple-element.124, f32[1408]{0:T(1024)S(1)} %get-tuple-element.6, ...), dimensions={0} | concatenate | bytes 8112896 | tf_op jit(solution)/shard_map/concatenate | solution.py:123
  99.6 4.3 %pad.13 = f32[1014272]{0:T(1024)} pad(f32[1014112]{0:T(1024)} %concatenate.3, f32[]{:T(128)} %constant.50.clone.1), padding=0_160 | pad | bytes 8113540 | tf_op jit(solution)/shard_map/jit(_pad)/pad | solution.py:211
  104.0 6.4 %reshape.178 = f32[32,31696]{1,0:T(8,128)} reshape(f32[1014272]{0:T(1024)} %pad.13) | data formatting | bytes 8114176 | tf_op jit(solution)/shard_map/reshape | solution.py:214
  112.0 2.1 fusion.100
  114.8 5.9 %all-to-all-start.1 = ((bf16[1,1,8,4,4,352]{5,4,3,1,0,2:T(4,128)(2,1)}), bf16[1,1,8,4,4,352]{5,4,3,1,0,2:T(4,128)(2,1)S(1)}, u32[]{:S(2)}, u32[]{:S(2)}) async-start(bf16[1,1,8,4,4,352]{5,4,3,1,0,2:T(4,128)(2,1)} %bitcast.19), calls=%async_computation.1 | async-start | bytes 196608 | tf_op jit(solution)/shard_map/all_to_all | solution.py:203
  120.8 1.7 fusion.2
  123.3 5.8 %all-to-all-done.1 = bf16[1,1,8,4,4,352]{5,4,3,1,0,2:T(4,128)(2,1)S(1)} async-done(((bf16[1,1,8,4,4,352]{5,4,3,1,0,2:T(4,128)(2,1)}), bf16[1,1,8,4,4,352]{5,4,3,1,0,2:T(4,128)(2,1)S(1)}, u32[]{:S(2)}, u32[]{:S(2)}) %all-to-all-start.1) | async-done | bytes 90144 | tf_op jit(solution)/shard_map/all_to_all | solution.py:203
  129.1 125.9 %all-reduce.6.cloned.1.call-done = f32[32,31696]{1,0:T(8,128)} async-done(((f32[32,31696]{1,0:T(8,128)}), f32[32,31696]{1,0:T(8,128)}) %all-reduce.6.cloned.1.call-update) | async-done | bytes 4057104
  255.1 2.0 dynamic-slice_multiply_fusion
  (271 shorter events, 20.0 us)
Async XLA Ops:
  7.2 31.9 %copy-start = (bf16[352,1408]{1,0:T(8,128)(2,1)S(1)}, bf16[352,1408]{1,0:T(8,128)(2,1)}, u32[]{:S(2)}) copy-start(bf16[352,1408]{1,0:T(8,128)(2,1)} %param.20) | copy-start | bytes 2973700
  7.2 31.5 %copy-start.84 = (f32[352]{0:T(512)S(1)}, f32[352]{0:T(512)}, u32[]{:S(2)}) copy-start(f32[352]{0:T(512)} %param.19) | copy-start | bytes 4228
  7.2 31.5 %copy-start.6 = (f32[352]{0:T(512)S(1)}, f32[352]{0:T(512)}, u32[]{:S(2)}) copy-start(f32[352]{0:T(512)} %param.18) | copy-start | bytes 4228
  7.2 31.8 %copy-start.81 = (f32[1408]{0:T(1024)S(1)}, f32[1408]{0:T(1024)}, u32[]{:S(2)}) copy-start(f32[1408]{0:T(1024)} %param.21) | copy-start | bytes 16900
  17.8 17.7 %all-to-all-start = ((bf16[8,1,1,1,4,4,352]{6,5,4,3,2,1,0:T(4,128)(2,1)}), bf16[8,1,1,1,4,4,352]{6,5,4,3,2,1,0:T(4,128)(2,1)S(1)}, u32[]{:S(2)}, u32[]{:S(2)}) async-start(bf16[8,1,1,1,4,4,352]{6,5,4,3,2,1,0:T(4,128)(2,1)} %constant_dynamic-update-slice_fusion), calls=%async_computation | async-start | bytes 196608 | tf_op jit(solution)/shard_map/all_to_all | solution.py:174
  25.1 230.0 %all-reduce.6.cloned.1.call-start = ((), (), s32[]{:S(2)}) async-start(), calls=%async_computation.2 | async-start | bytes 8126464
  26.1 12.3 %copy-start.7 = (f32[352]{0:T(512)}, f32[352]{0:T(512)S(1)}, u32[]{:S(2)}) copy-start(f32[352]{0:T(512)S(1)} %get-tuple-element.114) | copy-start | bytes 4228
  26.1 12.3 %copy-start.13 = (f32[352]{0:T(512)}, f32[352]{0:T(512)S(1)}, u32[]{:S(2)}) copy-start(f32[352]{0:T(512)S(1)} %get-tuple-element.117) | copy-start | bytes 4228
  26.1 14.0 %copy-start.9 = (f32[352]{0:T(512)}, f32[352]{0:T(512)S(1)}, u32[]{:S(2)}) copy-start(f32[352]{0:T(512)S(1)} %get-tuple-element.115) | copy-start | bytes 4228
  26.1 14.0 %copy-start.11 = (f32[352]{0:T(512)}, f32[352]{0:T(512)S(1)}, u32[]{:S(2)}) copy-start(f32[352]{0:T(512)S(1)} %get-tuple-element.116) | copy-start | bytes 4228
  26.1 14.0 %copy-start.15 = (f32[352]{0:T(512)}, f32[352]{0:T(512)S(1)}, u32[]{:S(2)}) copy-start(f32[352]{0:T(512)S(1)} %get-tuple-element.118) | copy-start | bytes 4228
  26.2 14.0 %copy-start.17 = (f32[352]{0:T(512)}, f32[352]{0:T(512)S(1)}, u32[]{:S(2)}) copy-start(f32[352]{0:T(512)S(1)} %get-tuple-element.119) | copy-start | bytes 4228
  26.2 14.0 %copy-start.19 = (f32[352]{0:T(512)}, f32[352]{0:T(512)S(1)}, u32[]{:S(2)}) copy-start(f32[352]{0:T(512)S(1)} %get-tuple-element.120) | copy-start | bytes 4228
  26.2 14.0 %copy-start.21 = (f32[352]{0:T(512)}, f32[352]{0:T(512)S(1)}, u32[]{:S(2)}) copy-start(f32[352]{0:T(512)S(1)} %get-tuple-element.121) | copy-start | bytes 4228
  26.2 14.0 %copy-start.23 = (f32[352]{0:T(512)}, f32[352]{0:T(512)S(1)}, u32[]{:S(2)}) copy-start(f32[352]{0:T(512)S(1)} %get-tuple-element.122) | copy-start | bytes 4228
  26.2 14.0 %copy-start.25 = (f32[352]{0:T(512)}, f32[352]{0:T(512)S(1)}, u32[]{:S(2)}) copy-start(f32[352]{0:T(512)S(1)} %get-tuple-element.123) | copy-start | bytes 4228
  27.5 11.3 %copy-start.35 = (f32[352]{0:T(512)}, f32[352]{0:T(512)S(1)}, u32[]{:S(2)}) copy-start(f32[352]{0:T(512)S(1)} %get-tuple-element.79) | copy-start | bytes 4228
  27.5 11.3 %copy-start.37 = (f32[352]{0:T(512)}, f32[352]{0:T(512)S(1)}, u32[]{:S(2)}) copy-start(f32[352]{0:T(512)S(1)} %get-tuple-element.80) | copy-start | bytes 4228
  27.5 11.3 %copy-start.39 = (f32[352]{0:T(512)}, f32[352]{0:T(512)S(1)}, u32[]{:S(2)}) copy-start(f32[352]{0:T(512)S(1)} %get-tuple-element.81) | copy-start | bytes 4228
  27.6 12.6 %copy-start.27 = (f32[352]{0:T(512)}, f32[352]{0:T(512)S(1)}, u32[]{:S(2)}) copy-start(f32[352]{0:T(512)S(1)} %get-tuple-element.75) | copy-start | bytes 4228
  27.6 12.6 %copy-start.29 = (f32[352]{0:T(512)}, f32[352]{0:T(512)S(1)}, u32[]{:S(2)}) copy-start(f32[352]{0:T(512)S(1)} %get-tuple-element.76) | copy-start | bytes 4228
  27.7 12.6 %copy-start.31 = (f32[352]{0:T(512)}, f32[352]{0:T(512)S(1)}, u32[]{:S(2)}) copy-start(f32[352]{0:T(512)S(1)} %get-tuple-element.77) | copy-start | bytes 4228
  27.7 12.6 %copy-start.33 = (f32[352]{0:T(512)}, f32[352]{0:T(512)S(1)}, u32[]{:S(2)}) copy-start(f32[352]{0:T(512)S(1)} %get-tuple-element.78) | copy-start | bytes 4228
  114.8 14.3 %all-to-all-start.1 = ((bf16[1,1,8,4,4,352]{5,4,3,1,0,2:T(4,128)(2,1)}), bf16[1,1,8,4,4,352]{5,4,3,1,0,2:T(4,128)(2,1)S(1)}, u32[]{:S(2)}, u32[]{:S(2)}) async-start(bf16[1,1,8,4,4,352]{5,4,3,1,0,2:T(4,128)(2,1)} %bitcast.19), calls=%async_computation.1 | async-start | bytes 196608 | tf_op jit(solution)/shard_map/all_to_all | solution.py:203
  (65 other events, 298.4 us)
Sparse Core Ops, SparseCore 0:
  110.8 144.1 all-reduce.5
